TPU v7x, 128 devices: a whole 4x4x4 slice. The times are simulated.
128 devices in a mesh: outer: 8 (over y, core), inner: 16 (over z, x).
Axes of the slice: x: 4, y: 4, z: 4, core: 2. Of those that a mesh axis runs over, the one named last changes fastest.
Arguments:
- layer_input: bfloat16 [16384, 7168], P(('outer', 'inner')), may hold values from -6 to 6
- out_grad: bfloat16 [16384, 7168], P(('outer', 'inner')), may hold values from -3 to 3
- expert_ids: int32 [16384, 8], P(('outer', 'inner')), may hold values from 0 to 255, as said below
- route_scales: float32 [16384, 8], P(('outer', 'inner')), may hold values from 0.25 to 2.5
- w_gate: bfloat16 [8, 7168, 2048], P('outer', None, 'inner'), may hold values from -0.0625 to 0.0625
- w_up: bfloat16 [8, 7168, 2048], P('outer', None, 'inner'), may hold values from -0.0625 to 0.0625
- w_down: bfloat16 [8, 2048, 7168], P('outer', 'inner'), may hold values from -0.125 to 0.125
Outputs:
- in_grad: bfloat16 [16384, 7168], P(('outer', 'inner'))
- grad_w_gate: float32 [8, 7168, 2048], P('outer', None, 'inner')
- grad_w_up: float32 [8, 7168, 2048], P('outer', None, 'inner')
- grad_w_down: float32 [8, 2048, 7168], P('outer', 'inner')
Inputs may be any that keep to these rules, and one draw needn't show every extreme that they name: `expert_ids`: each row names 8 different experts. In each device's aligned block of 128 rows at most 6 rows name any one expert below 8, and in every draw one expert below 8 is named by exactly 6 rows of every block.
All inputs are finite; a program needn't handle non-finite values.
Results may differ from a plain program's by a relative error of at most 0.014.
Values may be sent and summed in bfloat16 or wider, within the bound.
A program may use at most 192 MiB of HBM per device.

v0:
```python
import jax
import jax.numpy as jnp
from jax import lax
from jax.sharding import PartitionSpec as P

CAP = 6


def shards(layer_input, out_grad, expert_ids, route_scales, w_gate, w_up, w_down):
    tok_count = layer_input.shape[0]
    model_width = layer_input.shape[1]
    n_outer = lax.axis_size("outer")
    top_count = expert_ids.shape[1]
    slot_count = n_outer * CAP
    route_ids = expert_ids.reshape(-1)
    onehot = (route_ids[:, None] == jnp.arange(n_outer, dtype=jnp.int32)[None, :]).astype(jnp.int32)
    position = jnp.sum((jnp.cumsum(onehot, axis=0) - onehot) * onehot, axis=1)
    slot = jnp.where(route_ids < n_outer, route_ids * CAP + position, -1)
    picks = slot[:, None] == jnp.arange(slot_count, dtype=jnp.int32)[None, :]
    place = jnp.any(picks.reshape(tok_count, top_count, slot_count), axis=1).astype(jnp.bfloat16)
    slot_scale = jnp.sum(jnp.where(picks, route_scales.reshape(-1)[:, None], 0.0), axis=0)
    take_rows = (((0,), (0,)), ((), ()))
    send_x = lax.dot_general(
        place, layer_input, take_rows, preferred_element_type=jnp.float32
    ).astype(jnp.bfloat16)
    send_dy = lax.dot_general(place, out_grad, take_rows, preferred_element_type=jnp.float32)
    routed = (send_dy * slot_scale[:, None]).astype(jnp.bfloat16)
    send_x = send_x.reshape(n_outer, CAP, model_width)
    routed = routed.reshape(n_outer, CAP, model_width)
    gate_w = w_gate[0]
    up_w = w_up[0]
    down_w = w_down[0]
    got_x, got_gy = (
        lax.all_to_all(send_x, "outer", split_axis=0, concat_axis=0, tiled=True),
        lax.all_to_all(routed, "outer", split_axis=0, concat_axis=0, tiled=True),
    )
    rows_x = lax.all_gather(got_x.reshape(-1, model_width), "inner", axis=0, tiled=True)
    rows_gy = lax.all_gather(got_gy.reshape(-1, model_width), "inner", axis=0, tiled=True)
    gate = jnp.dot(rows_x, gate_w, preferred_element_type=jnp.float32)
    up_val = jnp.dot(rows_x, up_w, preferred_element_type=jnp.float32)
    sigmoid_gate = jax.nn.sigmoid(gate)
    silu_gate = gate * sigmoid_gate
    act = (silu_gate * up_val).astype(jnp.bfloat16)
    hid_grad = lax.dot_general(
        rows_gy, down_w, (((1,), (1,)), ((), ())), preferred_element_type=jnp.float32
    )
    gate_grad = (hid_grad * up_val * sigmoid_gate * (1.0 + gate * (1.0 - sigmoid_gate))).astype(
        jnp.bfloat16
    )
    up_grad = (hid_grad * silu_gate).astype(jnp.bfloat16)
    gate_sum = lax.dot_general(rows_x, gate_grad, take_rows, preferred_element_type=jnp.float32)
    up_sum = lax.dot_general(rows_x, up_grad, take_rows, preferred_element_type=jnp.float32)
    down_sum = lax.dot_general(act, rows_gy, take_rows, preferred_element_type=jnp.float32)
    gate_store = gate_grad
    up_store = up_grad
    carry = (gate_sum, up_sum, down_sum, gate_store, up_store)
    grad_gate, grad_up, grad_down, gate_store, up_store = carry
    term = lax.dot_general(
        gate_store, gate_w, (((1,), (1,)), ((), ())), preferred_element_type=jnp.float32
    )
    mine = lax.psum_scatter(
        (
            term
            + lax.dot_general(
                up_store, up_w, (((1,), (1,)), ((), ())), preferred_element_type=jnp.float32
            )
        ).astype(jnp.bfloat16),
        "inner",
        scatter_dimension=0,
        tiled=True,
    ).astype(jnp.float32)
    mine = mine.astype(jnp.bfloat16).reshape(n_outer, CAP, model_width)
    back = lax.all_to_all(mine, "outer", split_axis=0, concat_axis=0, tiled=True).reshape(
        slot_count, model_width
    )
    in_grad = jnp.dot(place, back, preferred_element_type=jnp.float32).astype(jnp.bfloat16)
    return (in_grad, grad_gate[None], grad_up[None], grad_down[None])


def solution(mesh):
    return jax.shard_map(
        shards,
        mesh=mesh,
        in_specs=(
            P(("outer", "inner"), None),
            P(("outer", "inner"), None),
            P(("outer", "inner"), None),
            P(("outer", "inner"), None),
            P("outer", None, "inner"),
            P("outer", None, "inner"),
            P("outer", "inner", None),
        ),
        out_specs=(
            P(("outer", "inner"), None),
            P("outer", None, "inner"),
            P("outer", None, "inner"),
            P("outer", "inner", None),
        ),
        check_vma=False,
    )
```

profile of v0, /device:TPU:1, one launch (start us, length us, event | category | flops | bytes accessed | tf_op | source)
XLA Modules:
  0.0 355.3 jit_solution(1478537319193128124)
XLA Ops:
  7.2 0.0 copy-start
  7.2 0.0 all-gather.5.cloned.1.call-start
  7.2 0.9 copy.27
  8.1 0.1 eq.45
  8.2 0.1 eq.49
  8.3 2.3 reduce-window.6
  10.6 0.3 slice_reduce_fusion
  10.9 0.2 reduce-window.9
  11.1 0.1 add_bitcast_fusion
  11.2 0.1 reduce_sum.21
  11.3 0.7 add_select_fusion.1
  12.0 0.0 copy-start.4
  12.1 1.9 convolution_convert_fusion.1
  14.0 0.2 reshape.72
  14.2 19.7 %all_to_all.15 = bf16[8,6,7168]{2,1,0:T(8,128)(2,1)} all-to-all(bf16[8,6,7168]{2,1,0:T(8,128)(2,1)S(1)} %reshape.72), channel_id=1, replica_groups=mesh['outer'=8,'inner'=16] {'outer'}, dimensions={0} | all-to-all | bytes 1376256 | tf_op jit(solution)/shard_map/all_to_all | solution.py:34
  33.9 2.3 reshape.73
  36.2 0.0 all-gather.5.cloned.1.call-update
  36.2 0.0 all-gather.3.cloned.1.call-start
  36.2 0.0 copy-done.4
  36.2 0.1 copy.30
  36.3 0.1 broadcast_in_dim.35
  36.4 0.1 select_reduce_fusion
  36.6 1.9 fusion
  38.5 0.2 reshape.70
  38.7 17.8 %all_to_all.16 = bf16[8,6,7168]{2,1,0:T(8,128)(2,1)} all-to-all(bf16[8,6,7168]{2,1,0:T(8,128)(2,1)S(1)} %reshape.70), channel_id=1, replica_groups=mesh['outer'=8,'inner'=16] {'outer'}, dimensions={0} | all-to-all | bytes 1376256 | tf_op jit(solution)/shard_map/all_to_all | solution.py:35
  56.5 2.3 reshape.71
  58.7 0.0 all-gather.3.cloned.1.call-update
  58.8 0.0 reduce-scatter.2.cloned.1.call-start
  58.8 61.0 %all-gather.5.cloned.1.call-done = bf16[768,7168]{1,0:T(8,128)(2,1)} async-done(((bf16[48,7168]{1,0:T(8,128)(2,1)}), bf16[768,7168]{1,0:T(8,128)(2,1)}) %all-gather.5.cloned.1.call-update) | async-done | bytes 11010064 | tf_op jit(solution)/shard_map/all_gather | solution.py:37
  119.8 0.0 copy-done
  119.8 0.0 copy-start.2
  119.8 0.0 copy-start.3
  119.8 7.2 %fusion.3 = f32[768,128]{1,0:T(8,128)S(1)} fusion(bf16[768,7168]{1,0:T(8,128)(2,1)} %all-gather.5.cloned.1.call-done, bf16[1,7168,128]{2,1,0:T(8,128)(2,1)S(1)} %copy-done), kind=kOutput, calls=%fused_computation.10 | convolution fusion | flops 1409286144 | bytes 13238272 | tf_op jit(solution)/shard_map/dot_general | solution.py:39
  127.0 0.1 copy-done.2
  127.1 0.5 copy-done.3
  127.6 3.0 fusion.6
  130.6 74.4 %all-gather.3.cloned.1.call-done = bf16[768,7168]{1,0:T(8,128)(2,1)} async-done(((bf16[48,7168]{1,0:T(8,128)(2,1)}), bf16[768,7168]{1,0:T(8,128)(2,1)}) %all-gather.3.cloned.1.call-update) | async-done | bytes 11010064 | tf_op jit(solution)/shard_map/all_gather | solution.py:38
  205.0 7.6 %multiply_convert_fusion.1 = (bf16[768,128]{1,0:T(8,128)(2,1)S(1)}, bf16[768,128]{1,0:T(8,128)(2,1)S(1)}) fusion(f32[768,128]{1,0:T(8,128)S(1)} %fusion.3, f32[768,128]{1,0:T(8,128)S(1)} %fusion.6, bf16[768,7168]{1,0:T(8,128)(2,1)} %all-gather.3.cloned.1.call-done, bf16[1,128,7168]{2,1,0:T(8,128)(2,1)} %param.13), kind=kOutput, calls=%fused_computation.18 | convolution fusion | flops 1410564096 | bytes 14024704 | tf_op jit(solution)/shard_map/dot_general | solution.py:44
  212.7 9.0 %fusion.1 = f32[768,7168]{1,0:T(8,128)} fusion(bf16[768,128]{1,0:T(8,128)(2,1)S(1)} %get-tuple-element.5, bf16[1,7168,128]{2,1,0:T(8,128)(2,1)S(1)} %copy-done), kind=kOutput, calls=%fused_computation.8 | convolution fusion | flops 1409286144 | bytes 24051712 | tf_op jit(solution)/shard_map/dot_general | solution.py:58
  221.7 13.2 %add_convert_fusion = bf16[768,7168]{1,0:T(8,128)(2,1)} fusion(f32[768,7168]{1,0:T(8,128)} %fusion.1, bf16[768,128]{1,0:T(8,128)(2,1)S(1)} %get-tuple-element.4, bf16[1,7168,128]{2,1,0:T(8,128)(2,1)} %param.12), kind=kOutput, calls=%fused_computation | convolution fusion | flops 1420296192 | bytes 35061760 | tf_op jit(solution)/shard_map/dot_general | solution.py:64
  234.9 0.0 reduce-scatter.2.cloned.1.call-update
  234.9 9.0 %convolution_bitcast_fusion.1 = f32[1,7168,128]{2,1,0:T(8,128)} fusion(bf16[768,7168]{1,0:T(8,128)(2,1)} %all-gather.5.cloned.1.call-done, bf16[768,128]{1,0:T(8,128)(2,1)S(1)} %get-tuple-element.4), kind=kOutput, calls=%fused_computation.2 | convolution fusion | flops 1409286144 | bytes 14876672 | tf_op jit(solution)/shard_map/dot_general | solution.py:52
  243.9 9.2 %convolution_bitcast_fusion.2 = f32[1,7168,128]{2,1,0:T(8,128)} fusion(bf16[768,7168]{1,0:T(8,128)(2,1)} %all-gather.5.cloned.1.call-done, bf16[768,128]{1,0:T(8,128)(2,1)S(1)} %get-tuple-element.5), kind=kOutput, calls=%fused_computation.3 | convolution fusion | flops 1409286144 | bytes 14876672 | tf_op jit(solution)/shard_map/dot_general | solution.py:51
  253.1 72.1 %reduce-scatter.2.cloned.1.call-done = bf16[48,7168]{1,0:T(8,128)(2,1)} async-done(((bf16[768,7168]{1,0:T(8,128)(2,1)}), bf16[48,7168]{1,0:T(8,128)(2,1)}) %reduce-scatter.2.cloned.1.call-update) | async-done | bytes 688144 | tf_op jit(solution)/shard_map/reduce_scatter | solution.py:61
  325.1 2.3 reshape.74
  327.4 5.5 %all-to-all-start.2 = ((bf16[8,6,7168]{2,1,0:T(8,128)(2,1)}), bf16[8,6,7168]{2,1,0:T(8,128)(2,1)S(1)}, u32[]{:S(2)}, u32[]{:S(2)}) async-start(bf16[8,6,7168]{2,1,0:T(8,128)(2,1)} %reshape.74), calls=%async_computation.3 | async-start | bytes 1835008 | tf_op jit(solution)/shard_map/all_to_all | solution.py:73
  332.9 0.0 copy-start.1
  332.9 7.8 %convolution_bitcast_fusion = f32[1,128,7168]{2,1,0:T(8,128)} fusion(bf16[768,7168]{1,0:T(8,128)(2,1)} %all-gather.3.cloned.1.call-done, f32[768,128]{1,0:T(8,128)S(1)} %fusion.6, f32[768,128]{1,0:T(8,128)S(1)} %fusion.3), kind=kOutput, calls=%fused_computation.1 | convolution fusion | flops 1409875968 | bytes 15466496 | tf_op jit(solution)/shard_map/dot_general | solution.py:53
  340.7 5.9 %all-to-all-done.2 = bf16[8,6,7168]{2,1,0:T(8,128)(2,1)S(1)} async-done(((bf16[8,6,7168]{2,1,0:T(8,128)(2,1)}), bf16[8,6,7168]{2,1,0:T(8,128)(2,1)S(1)}, u32[]{:S(2)}, u32[]{:S(2)}) %all-to-all-start.2) | async-done | bytes 688160 | tf_op jit(solution)/shard_map/all_to_all | solution.py:73
  346.6 0.3 reshape.75
  346.8 1.9 convolution_convert_fusion
  348.7 0.0 copy-done.1
  (5 shorter events, 0.1 us)
Async XLA Ops:
  7.2 112.6 %copy-start = (bf16[1,7168,128]{2,1,0:T(8,128)(2,1)S(1)}, bf16[1,7168,128]{2,1,0:T(8,128)(2,1)}, u32[]{:S(2)}) copy-start(bf16[1,7168,128]{2,1,0:T(8,128)(2,1)} %param.11) | copy-start | bytes 5505028
  7.2 112.6 %all-gather.5.cloned.1.call-start = ((), (), s32[]{:S(2)}) async-start(), calls=%async_computation.5 | async-start | bytes 11698176 | tf_op jit(solution)/shard_map/all_gather | solution.py:37
  12.0 24.2 %copy-start.4 = (f32[128,8]{0,1:T(8,128)S(1)}, f32[128,8]{0,1:T(8,128)}, u32[]{:S(2)}) copy-start(f32[128,8]{0,1:T(8,128)} %param.10) | copy-start | bytes 12292
  36.2 168.8 %all-gather.3.cloned.1.call-start = ((), (), s32[]{:S(2)}) async-start(), calls=%async_computation.4 | async-start | bytes 11698176 | tf_op jit(solution)/shard_map/all_gather | solution.py:38
  58.8 266.4 %reduce-scatter.2.cloned.1.call-start = ((), (), s32[]{:S(2)}) async-start(), calls=%async_computation.6 | async-start | bytes 11698176 | tf_op jit(solution)/shard_map/reduce_scatter | solution.py:61
  119.8 7.3 %copy-start.2 = (bf16[768,7168]{1,0:T(8,128)(2,1)S(1)}, bf16[768,7168]{1,0:T(8,128)(2,1)}, u32[]{:S(2)}) copy-start(bf16[768,7168]{1,0:T(8,128)(2,1)} %all-gather.5.cloned.1.call-done) | copy-start | bytes 33030148
  119.8 7.8 %copy-start.3 = (bf16[1,7168,128]{2,1,0:T(8,128)(2,1)S(1)}, bf16[1,7168,128]{2,1,0:T(8,128)(2,1)}, u32[]{:S(2)}) copy-start(bf16[1,7168,128]{2,1,0:T(8,128)(2,1)} %param.12) | copy-start | bytes 5505028
  327.4 19.2 %all-to-all-start.2 = ((bf16[8,6,7168]{2,1,0:T(8,128)(2,1)}), bf16[8,6,7168]{2,1,0:T(8,128)(2,1)S(1)}, u32[]{:S(2)}, u32[]{:S(2)}) async-start(bf16[8,6,7168]{2,1,0:T(8,128)(2,1)} %reshape.74), calls=%async_computation.3 | async-start | bytes 1835008 | tf_op jit(solution)/shard_map/all_to_all | solution.py:73
  332.9 15.9 %copy-start.1 = (bf16[1,7168,128]{2,1,0:T(8,128)(2,1)S(1)}, bf16[1,7168,128]{2,1,0:T(8,128)(2,1)}, u32[]{:S(2)}) copy-start(bf16[1,7168,128]{2,1,0:T(8,128)(2,1)} %param.11) | copy-start | bytes 5505028
Sparse Core Ops, SparseCore 0:
  36.3 83.4 all-gather.4
  122.5 82.4 all-gather.2
  235.0 90.0 reduce-scatter.1
where the time goes:
time: 356 us; the launch traced here: 355 us
  waiting for transfers between devices  213 us (60%)
  matrix products  71.7 us (20%)
  blocking collectives  37.4 us (11%)
  between operations  13.9 us (4%)
  local copies, waits for them, and re-layouts  9.88 us (3%)
  starting transfers between devices  5.58 us (2%)
    all_gather x1, waiting for transfers between devices, shards(): lax.all_gather(got_gy.reshape(-1, model_width), 'inner', axis=0, tiled=True)  74.4 us
    reduce_scatter x1, waiting for transfers between devices, shards(): lax.psum_scatter((term + lax.dot_general(up_store, up_w, (((1,), (1,)), (...  72.1 us
    all_gather x1, waiting for transfers between devices, shards(): lax.all_gather(got_x.reshape(-1, model_width), 'inner', axis=0, tiled=True)  61 us
    all_to_all x1, blocking collectives, shards(): lax.all_to_all(send_x, 'outer', split_axis=0, concat_axis=0, tiled=True)  19.7 us
    all_to_all x1, blocking collectives, shards(): lax.all_to_all(routed, 'outer', split_axis=0, concat_axis=0, tiled=True)  17.8 us
    dot_general x1, matrix products, shards(): lax.dot_general(up_store, up_w, (((1,), (1,)), ((), ())), preferred_eleme...  13.2 us
    dot_general x1, matrix products, shards(): lax.dot_general(rows_x, gate_grad, take_rows, preferred_element_type=jnp....  9.15 us
    dot_general x1, matrix products, shards(): lax.dot_general(rows_x, up_grad, take_rows, preferred_element_type=jnp.fl...  9.03 us
  transfers between devices with their start and end apart: 4, of which 4 were waited for; matrix products, arithmetic and copies ran while one was open for 12% of the time, Pallas kernels for 0%

commit v1 on v0

--- a/solution.py
+++ b/solution.py
@@ -34,7 +34,11 @@
         lax.all_to_all(send_x, "outer", split_axis=0, concat_axis=0, tiled=True),
         lax.all_to_all(routed, "outer", split_axis=0, concat_axis=0, tiled=True),
     )
-    rows_x = lax.all_gather(got_x.reshape(-1, model_width), "inner", axis=0, tiled=True)
+    z_in = got_x.reshape(-1, model_width)
+    windows = []
+    for _ in range(lax.psum(1, "inner")):
+        windows.append(z_in)
+    rows_x = jnp.concatenate(lax.all_to_all(jnp.stack(windows, axis=0), "inner", 0, 0), axis=0)
     rows_gy = lax.all_gather(got_gy.reshape(-1, model_width), "inner", axis=0, tiled=True)
     gate = jnp.dot(rows_x, gate_w, preferred_element_type=jnp.float32)
     up_val = jnp.dot(rows_x, up_w, preferred_element_type=jnp.float32)

time: 356 us -> 395 us (1.11)
  blocking collectives: 37.4 us -> 213 us
  waiting for transfers between devices: 213 us -> 74.2 us
  local copies, waits for them, and re-layouts: 9.88 us -> 16 us
  matrix products: 71.7 us -> 67.6 us
    all_to_all x0 -> x1, blocking collectives: none -> 176 us  [shards(): lax.all_to_all(jnp.stack(windows, axis=0), 'inner', 0, 0)]
    all_gather x1, waiting for transfers between devices: 74.4 us -> 0.02 us  [shards(): lax.all_gather(got_gy.reshape(-1, model_width), 'inner', axis=0, tiled=True)]
    all_gather x1 -> x0, waiting for transfers between devices: 61 us -> none  [shards(): lax.all_gather(got_x.reshape(-1, model_width), 'inner', axis=0, tiled=True)]
    another operation x0 -> x2, local copies, waits for them, and re-layouts: none -> 6.97 us  [shards(): jnp.stack(windows, axis=0)]
    dot_general x1, matrix products: 7.22 us -> 2.99 us  [shards(): gate = jnp.dot(rows_x, gate_w, preferred_element_type=jnp.float32)]
  transfers between devices with their start and end apart: 4 -> 3, of which waited for: 4 -> 2; matrix products, arithmetic and copies ran while one was open for 12% -> 10% of each run, Pallas kernels for 0% -> 0%
where the time goes in v1:
time: 395 us; the launch traced here: 394 us
  blocking collectives  213 us (54%)
  waiting for transfers between devices  74.2 us (19%)
  matrix products  67.6 us (17%)
  local copies, waits for them, and re-layouts  16 us (4%)
  between operations  14.2 us (4%)
  starting transfers between devices  5.63 us (1%)
    all_to_all x1, blocking collectives, shards(): lax.all_to_all(jnp.stack(windows, axis=0), 'inner', 0, 0)  176 us
    reduce_scatter x1, waiting for transfers between devices, shards(): lax.psum_scatter((term + lax.dot_general(up_store, up_w, (((1,), (1,)), (...  68.3 us
    all_to_all x1, blocking collectives, shards(): lax.all_to_all(routed, 'outer', split_axis=0, concat_axis=0, tiled=True)  19.7 us
    all_to_all x1, blocking collectives, shards(): lax.all_to_all(send_x, 'outer', split_axis=0, concat_axis=0, tiled=True)  17.8 us
    dot_general x1, matrix products, shards(): lax.dot_general(up_store, up_w, (((1,), (1,)), ((), ())), preferred_eleme...  13.2 us
    dot_general x1, matrix products, shards(): lax.dot_general(rows_x, gate_grad, take_rows, preferred_element_type=jnp....  9.19 us
    dot_general x1, matrix products, shards(): lax.dot_general(rows_x, up_grad, take_rows, preferred_element_type=jnp.fl...  9.03 us
    dot_general x1, matrix products, shards(): lax.dot_general(gate_store, gate_w, (((1,), (1,)), ((), ())), preferred_e...  9.02 us
  transfers between devices with their start and end apart: 3, of which 2 were waited for; matrix products, arithmetic and copies ran while one was open for 10% of the time, Pallas kernels for 0%

profile of v1, /device:TPU:1, one launch (start us, length us, event | category | flops | bytes accessed | tf_op | source)
XLA Modules:
  0.0 394.0 jit_solution(2562316342508416544)
XLA Ops:
  7.2 0.0 copy-start
  7.2 0.0 all-gather.2.cloned.1.call-start
  7.2 0.9 copy.27
  8.1 0.1 eq.45
  8.2 0.1 eq.49
  8.3 2.3 reduce-window.6
  10.6 0.3 slice_reduce_fusion
  10.9 0.2 reduce-window.9
  11.1 0.1 add_bitcast_fusion
  11.2 0.1 reduce_sum.21
  11.3 0.7 add_select_fusion.1
  12.1 0.8 copy.30
  12.9 0.1 broadcast_in_dim.35
  12.9 0.1 select_reduce_fusion
  13.1 1.9 fusion
  15.0 0.2 reshape.72
  15.2 19.7 %all_to_all.20 = bf16[8,6,7168]{2,1,0:T(8,128)(2,1)} all-to-all(bf16[8,6,7168]{2,1,0:T(8,128)(2,1)S(1)} %reshape.72), channel_id=1, replica_groups=mesh['outer'=8,'inner'=16] {'outer'}, dimensions={0} | all-to-all | bytes 1376256 | tf_op jit(solution)/shard_map/all_to_all | solution.py:35
  34.9 2.3 reshape.73
  37.2 0.0 all-gather.2.cloned.1.call-update
  37.2 0.0 reduce-scatter.2.cloned.1.call-start
  37.2 1.9 convolution_convert_fusion.1
  39.1 0.2 reshape.74
  39.4 17.8 %all_to_all.21 = bf16[8,6,7168]{2,1,0:T(8,128)(2,1)} all-to-all(bf16[8,6,7168]{2,1,0:T(8,128)(2,1)S(1)} %reshape.74), channel_id=1, replica_groups=mesh['outer'=8,'inner'=16] {'outer'}, dimensions={0} | all-to-all | bytes 1376256 | tf_op jit(solution)/shard_map/all_to_all | solution.py:34
  57.1 1.4 stack_reshape.2
  58.6 5.5 %stack.3 = bf16[16,48,7168]{2,1,0:T(8,128)(2,1)} broadcast(bf16[48,7168]{1,0:T(8,128)(2,1)S(1)} %stack_reshape.2), dimensions={1,2} | broadcast | bytes 11698176 | tf_op jit(solution)/shard_map/stack | solution.py:41
  64.1 175.7 %all_to_all.22 = bf16[16,48,7168]{2,1,0:T(8,128)(2,1)S(1)} all-to-all(bf16[16,48,7168]{2,1,0:T(8,128)(2,1)} %stack.3), channel_id=1, replica_groups=mesh['outer'=8,'inner'=16] {'inner'}, dimensions={0} | all-to-all | bytes 22020096 | tf_op jit(solution)/shard_map/all_to_all | solution.py:41
  239.8 0.0 copy-start.2
  239.8 0.0 copy-done
  239.8 0.0 copy-start.3
  239.8 3.0 fusion.3
  242.8 1.3 copy-done.2
  244.1 0.0 copy-done.3
  244.1 3.0 fusion.6
  247.1 0.0 all-gather.2.cloned.1.call-done
  247.1 7.6 %multiply_convert_fusion.1 = (bf16[768,128]{1,0:T(8,128)(2,1)S(1)}, bf16[768,128]{1,0:T(8,128)(2,1)S(1)}) fusion(f32[768,128]{1,0:T(8,128)S(1)} %fusion.3, f32[768,128]{1,0:T(8,128)S(1)} %fusion.6, bf16[768,7168]{1,0:T(8,128)(2,1)} %all-gather.2.cloned.1.call-done, bf16[1,128,7168]{2,1,0:T(8,128)(2,1)} %param.13), kind=kOutput, calls=%fused_computation.18 | convolution fusion | flops 1410564096 | bytes 14024704 | tf_op jit(solution)/shard_map/dot_general | solution.py:48
  254.8 9.0 %fusion.1 = f32[768,7168]{1,0:T(8,128)} fusion(bf16[768,128]{1,0:T(8,128)(2,1)S(1)} %get-tuple-element.5, bf16[1,7168,128]{2,1,0:T(8,128)(2,1)S(1)} %copy-done), kind=kOutput, calls=%fused_computation.8 | convolution fusion | flops 1409286144 | bytes 24051712 | tf_op jit(solution)/shard_map/dot_general | solution.py:62
  263.8 13.2 %add_convert_fusion = bf16[768,7168]{1,0:T(8,128)(2,1)} fusion(f32[768,7168]{1,0:T(8,128)} %fusion.1, bf16[768,128]{1,0:T(8,128)(2,1)S(1)} %get-tuple-element.4, bf16[1,7168,128]{2,1,0:T(8,128)(2,1)} %param.12), kind=kOutput, calls=%fused_computation | convolution fusion | flops 1420296192 | bytes 35061760 | tf_op jit(solution)/shard_map/dot_general | solution.py:68
  277.0 0.0 reduce-scatter.2.cloned.1.call-update
  277.0 9.0 %convolution_bitcast_fusion.1 = f32[1,7168,128]{2,1,0:T(8,128)} fusion(bf16[768,7168]{1,0:T(8,128)(2,1)} %bitcast.59, bf16[768,128]{1,0:T(8,128)(2,1)S(1)} %get-tuple-element.4), kind=kOutput, calls=%fused_computation.2 | convolution fusion | flops 1409286144 | bytes 14876672 | tf_op jit(solution)/shard_map/dot_general | solution.py:56
  286.0 9.2 %convolution_bitcast_fusion.2 = f32[1,7168,128]{2,1,0:T(8,128)} fusion(bf16[768,7168]{1,0:T(8,128)(2,1)} %bitcast.60, bf16[768,128]{1,0:T(8,128)(2,1)S(1)} %get-tuple-element.5), kind=kOutput, calls=%fused_computation.3 | convolution fusion | flops 1409286144 | bytes 14876672 | tf_op jit(solution)/shard_map/dot_general | solution.py:55
  295.2 68.3 %reduce-scatter.2.cloned.1.call-done = bf16[48,7168]{1,0:T(8,128)(2,1)} async-done(((bf16[768,7168]{1,0:T(8,128)(2,1)}), bf16[48,7168]{1,0:T(8,128)(2,1)}) %reduce-scatter.2.cloned.1.call-update) | async-done | bytes 688144 | tf_op jit(solution)/shard_map/reduce_scatter | solution.py:65
  363.5 2.3 reshape.76
  365.8 5.6 %all-to-all-start.3 = ((bf16[8,6,7168]{2,1,0:T(8,128)(2,1)}), bf16[8,6,7168]{2,1,0:T(8,128)(2,1)S(1)}, u32[]{:S(2)}, u32[]{:S(2)}) async-start(bf16[8,6,7168]{2,1,0:T(8,128)(2,1)} %reshape.76), calls=%async_computation.4 | async-start | bytes 1835008 | tf_op jit(solution)/shard_map/all_to_all | solution.py:77
  371.3 0.0 copy-start.1
  371.3 7.8 %convolution_bitcast_fusion = f32[1,128,7168]{2,1,0:T(8,128)} fusion(bf16[768,7168]{1,0:T(8,128)(2,1)} %all-gather.2.cloned.1.call-done, f32[768,128]{1,0:T(8,128)S(1)} %fusion.6, f32[768,128]{1,0:T(8,128)S(1)} %fusion.3), kind=kOutput, calls=%fused_computation.1 | convolution fusion | flops 1409875968 | bytes 15466496 | tf_op jit(solution)/shard_map/dot_general | solution.py:57
  379.1 5.9 %all-to-all-done.3 = bf16[8,6,7168]{2,1,0:T(8,128)(2,1)S(1)} async-done(((bf16[8,6,7168]{2,1,0:T(8,128)(2,1)}), bf16[8,6,7168]{2,1,0:T(8,128)(2,1)S(1)}, u32[]{:S(2)}, u32[]{:S(2)}) %all-to-all-start.3) | async-done | bytes 688160 | tf_op jit(solution)/shard_map/all_to_all | solution.py:77
  385.0 0.3 reshape.77
  385.3 1.9 convolution_convert_fusion
  387.2 0.0 copy-done.1
  (5 shorter events, 0.1 us)
Async XLA Ops:
  7.2 232.6 %copy-start = (bf16[1,7168,128]{2,1,0:T(8,128)(2,1)S(1)}, bf16[1,7168,128]{2,1,0:T(8,128)(2,1)}, u32[]{:S(2)}) copy-start(bf16[1,7168,128]{2,1,0:T(8,128)(2,1)} %param.11) | copy-start | bytes 5505028
  7.2 239.9 %all-gather.2.cloned.1.call-start = ((), (), s32[]{:S(2)}) async-start(), calls=%async_computation.5 | async-start | bytes 11698176 | tf_op jit(solution)/shard_map/all_gather | solution.py:42
  37.2 326.3 %reduce-scatter.2.cloned.1.call-start = ((), (), s32[]{:S(2)}) async-start(), calls=%async_computation.6 | async-start | bytes 11698176 | tf_op jit(solution)/shard_map/reduce_scatter | solution.py:65
  239.8 4.3 %copy-start.2 = (bf16[16,48,7168]{2,1,0:T(8,128)(2,1)}, bf16[16,48,7168]{2,1,0:T(8,128)(2,1)S(1)}, u32[]{:S(2)}) copy-start(bf16[16,48,7168]{2,1,0:T(8,128)(2,1)S(1)} %all_to_all.22) | copy-start | bytes 33030148
  239.8 4.3 %copy-start.3 = (bf16[1,7168,128]{2,1,0:T(8,128)(2,1)S(1)}, bf16[1,7168,128]{2,1,0:T(8,128)(2,1)}, u32[]{:S(2)}) copy-start(bf16[1,7168,128]{2,1,0:T(8,128)(2,1)} %param.12) | copy-start | bytes 5505028
  365.8 19.2 %all-to-all-start.3 = ((bf16[8,6,7168]{2,1,0:T(8,128)(2,1)}), bf16[8,6,7168]{2,1,0:T(8,128)(2,1)S(1)}, u32[]{:S(2)}, u32[]{:S(2)}) async-start(bf16[8,6,7168]{2,1,0:T(8,128)(2,1)} %reshape.76), calls=%async_computation.4 | async-start | bytes 1835008 | tf_op jit(solution)/shard_map/all_to_all | solution.py:77
  371.3 15.9 %copy-start.1 = (bf16[1,7168,128]{2,1,0:T(8,128)(2,1)S(1)}, bf16[1,7168,128]{2,1,0:T(8,128)(2,1)}, u32[]{:S(2)}) copy-start(bf16[1,7168,128]{2,1,0:T(8,128)(2,1)} %param.11) | copy-start | bytes 5505028
Sparse Core Ops, SparseCore 0:
  37.3 196.1 all-gather.1
  277.1 86.3 reduce-scatter.1
